TPU v7x, 256 devices: a whole 4x4x8 slice. The times are simulated.
256 devices in a mesh: ex: 16 (over y_hi, z), feat: 16 (over x, y_lo, core).
Axes of the slice: x: 4, y: 4 (y_hi: 2, y_lo: 2; y = y_hi * 2 + y_lo), z: 8, core: 2. Of those that a mesh axis runs over, the one named last changes fastest.
Arguments:
- grads: float32 [16384, 32768], P('ex', 'feat'), may hold values from -0.44595265 to 0.44595265
- resid: float32 [16384], P('ex'), may hold values from 0.1 to 1
- offsets: int32 [3], replicated, may hold values from 0 to 512
Outputs:
- kernel: float32 [3, 512, 16384], P(None, 'feat', 'ex')
All inputs are finite; a program needn't handle non-finite values.
Results may differ from a plain program's by a relative error of at most 0.00015.
Values sent between devices are 32-bit elements; how exact they have to be, the bound alone decides.
A program may use at most 64 MiB of HBM per device.

v0:
```python
import jax
import jax.numpy as jnp
from jax import lax
from jax.sharding import PartitionSpec as P

GROUP = 512
STEPS = 3


def shifted(value, axis, steps):
    count = lax.axis_size(axis)
    pairs = [(source, (source + steps) % count) for source in range(count)]
    return lax.ppermute(value, axis, pairs)


def shards(grads, resid, offsets):
    blocks = []
    block_ws = []
    for step in range(STEPS):
        start = offsets[step]
        blocks.append(lax.dynamic_slice_in_dim(grads, start, GROUP, 0))
        block_ws.append(lax.dynamic_slice_in_dim(resid, start, GROUP, 0))
    visitors = []
    visitor_ws = []
    for step in range(STEPS):
        got, got_w = shifted((blocks[step], block_ws[step]), "ex", step + 1)
        visitors.append(got)
        visitor_ws.append(got_w)
    count = GROUP // lax.axis_size("feat")
    first = lax.axis_index("feat") * count
    results = []
    for step in range(STEPS):
        visitor = visitors[step]
        partial_tile = lax.dot_general(
            visitor,
            grads,
            (((1,), (1,)), ((), ())),
            precision=lax.Precision.HIGHEST,
            preferred_element_type=jnp.float32,
        )
        total = lax.psum(partial_tile, "feat")
        mine = lax.dynamic_slice_in_dim(total, first, count, 0)
        mine_w = lax.dynamic_slice_in_dim(visitor_ws[step], first, count, 0)
        results.append(mine * mine * mine_w[:, None] * resid[None, :])
    return jnp.stack(results)


def solution(mesh):
    return jax.shard_map(
        shards,
        mesh=mesh,
        in_specs=(P("ex", "feat"), P("ex"), P()),
        out_specs=P(None, "feat", "ex"),
        check_vma=False,
    )
```

profile of v0, /device:TPU:1, one launch (start us, length us, event | category | flops | bytes accessed | tf_op | source)
XLA Modules:
  0.0 756.1 jit_solution(4774046644589135644)
XLA Ops:
  6.5 0.0 all-reduce.3.cloned.1.call-start
  6.5 1.4 fusion.1
  13.6 10.4 %constant_dynamic-slice_fusion.2 = (f32[512,2048]{1,0:T(8,128)}, f32[512,2048]{1,0:T(8,128)}, f32[512,2048]{1,0:T(8,128)S(1)}) fusion(f32[1024,2048]{1,0:T(8,128)} %param.3, s32[]{:T(128)S(6)} %select_n.8, s32[]{:T(128)S(6)} %select_n.10, s32[]{:T(128)S(6)} %select_n.11), kind=kLoop, calls=%fused_computation.6 | loop fusion | bytes 25165836 | tf_op jit(solution)/shard_map/dynamic_slice | solution.py:21
  24.0 2.5 collective-permute-start
  26.5 3.0 collective-permute-start.2
  29.5 0.0 slice-start
  29.5 0.0 slice-start.1
  29.5 3.8 collective-permute-start.4
  33.2 90.3 %collective-permute-done = f32[512,2048]{1,0:T(8,128)S(1)} collective-permute-done((f32[512,2048]{1,0:T(8,128)}, f32[512,2048]{1,0:T(8,128)S(1)}, u32[]{:S(2)}, u32[]{:S(2)}) %collective-permute-start) | collective-permute-done | bytes 4194336 | tf_op jit(solution)/shard_map/ppermute | solution.py:13
  123.5 17.2 %fusion.2 = f32[512,1024]{1,0:T(8,128)} fusion(f32[512,2048]{1,0:T(8,128)S(1)} %collective-permute-done, f32[1024,2048]{1,0:T(8,128)} %param.3), kind=kOutput, calls=%fused_computation.9 | convolution fusion | flops 12884901888 | bytes 14680064 | tf_op jit(solution)/shard_map/dot_general | solution.py:34
  140.8 74.7 %collective-permute-done.2 = f32[512,2048]{1,0:T(8,128)S(1)} collective-permute-done((f32[512,2048]{1,0:T(8,128)}, f32[512,2048]{1,0:T(8,128)S(1)}, u32[]{:S(2)}, u32[]{:S(2)}) %collective-permute-start.2) | collective-permute-done | bytes 4194336 | tf_op jit(solution)/shard_map/ppermute | solution.py:13
  215.5 0.0 slice-done
  215.5 0.0 slice-done.1
  215.5 15.3 %fusion.3 = f32[512,1024]{1,0:T(8,128)} fusion(f32[512,2048]{1,0:T(8,128)S(1)} %collective-permute-done.2, f32[1024,2048]{1,0:T(8,128)S(1)} %bitcast.16), kind=kOutput, calls=%fused_computation.10 | convolution fusion | flops 12884901888 | bytes 14680064 | tf_op jit(solution)/shard_map/dot_general | solution.py:34
  230.8 341.8 %collective-permute-done.4 = f32[512,2048]{1,0:T(8,128)S(1)} collective-permute-done((f32[512,2048]{1,0:T(8,128)S(1)}, f32[512,2048]{1,0:T(8,128)S(1)}, u32[]{:S(2)}, u32[]{:S(2)}) %collective-permute-start.4) | collective-permute-done | bytes 4194336 | tf_op jit(solution)/shard_map/ppermute | solution.py:13
  572.6 15.3 %fusion.4 = f32[512,1024]{1,0:T(8,128)} fusion(f32[512,2048]{1,0:T(8,128)S(1)} %collective-permute-done.4, f32[1024,2048]{1,0:T(8,128)S(1)} %bitcast.16), kind=kOutput, calls=%fused_computation.11 | convolution fusion | flops 12884901888 | bytes 14680064 | tf_op jit(solution)/shard_map/dot_general | solution.py:34
  587.9 0.0 copy-start
  587.9 0.0 all-reduce.3.cloned.1.call-update
  588.0 0.7 copy-done
  588.6 0.1 fusion
  588.7 2.5 collective-permute-start.1
  591.2 0.0 collective-permute-start.3
  591.2 1.3 collective-permute-start.5
  592.5 2.3 collective-permute-done.1
  594.8 0.1 dynamic_slice.39
  594.8 3.3 collective-permute-done.3
  598.1 0.1 dynamic_slice.43
  598.2 0.9 collective-permute-done.5
  599.0 0.1 dynamic_slice.47
  599.1 147.8 %all-reduce.3.cloned.1.call-done = (f32[512,1024]{1,0:T(8,128)}, f32[512,1024]{1,0:T(8,128)}, f32[512,1024]{1,0:T(8,128)}) async-done(((f32[512,1024]{1,0:T(8,128)}, f32[512,1024]{1,0:T(8,128)}, f32[512,1024]{1,0:T(8,128)}), (f32[512,1024]{1,0:T(8,128)}, f32[512,1024]{1,0:T(8,128)}, f32[512,1024]{1,0:T(8,128)})) %all-reduce.3.cloned.1.call-update) | async-done | bytes 6291472 | tf_op jit(solution)/shard_map/psum | solution.py:41
  746.9 1.1 multiply_bitcast_fusion.2
  748.0 0.8 pad_maximum_fusion
  (1 shorter events, 0.0 us)
Async XLA Ops:
  6.5 740.4 %all-reduce.3.cloned.1.call-start = ((), (), s32[]{:S(2)}) async-start(), calls=%async_computation | async-start | bytes 12582912 | tf_op jit(solution)/shard_map/psum | solution.py:41
  24.0 99.5 %collective-permute-start = (f32[512,2048]{1,0:T(8,128)}, f32[512,2048]{1,0:T(8,128)S(1)}, u32[]{:S(2)}, u32[]{:S(2)}) collective-permute-start(f32[512,2048]{1,0:T(8,128)} %get-tuple-element.8), channel_id=1, source_target_pairs={{0,16},{16,32},{32,48},{48,64},{64,80},{80,96},{96,112},{112,128},... | collective-permute-start | bytes 12582920 | tf_op jit(solution)/shard_map/ppermute | solution.py:13
  26.5 189.1 %collective-permute-start.2 = (f32[512,2048]{1,0:T(8,128)}, f32[512,2048]{1,0:T(8,128)S(1)}, u32[]{:S(2)}, u32[]{:S(2)}) collective-permute-start(f32[512,2048]{1,0:T(8,128)} %get-tuple-element.9), channel_id=1, source_target_pairs={{0,32},{16,48},{32,64},{48,80},{64,96},{80,112},{96,128},{112,144}... | collective-permute-start | bytes 12582920 | tf_op jit(solution)/shard_map/ppermute | solution.py:13
  29.5 186.1 %slice-start = ((s8[8388608]{0:T(1024)(128)(4,1)}), s8[4194304]{0:T(1024)(128)(4,1)S(1)}, s32[]{:S(2)}) async-start(s8[8388608]{0:T(1024)(128)(4,1)} %bitcast.15), calls=%async_computation.1 | async-start | bytes 8388608
  29.5 186.1 %slice-start.1 = ((s8[8388608]{0:T(1024)(128)(4,1)}), s8[4194304]{0:T(1024)(128)(4,1)S(1)}, s32[]{:S(2)}) async-start(s8[8388608]{0:T(1024)(128)(4,1)} %bitcast.15), calls=%async_computation.2 | async-start | bytes 8388608
  29.5 543.1 %collective-permute-start.4 = (f32[512,2048]{1,0:T(8,128)S(1)}, f32[512,2048]{1,0:T(8,128)S(1)}, u32[]{:S(2)}, u32[]{:S(2)}) collective-permute-start(f32[512,2048]{1,0:T(8,128)S(1)} %get-tuple-element.10), channel_id=1, source_target_pairs={{0,48},{16,64},{32,80},{48,96},{64,112},{80,128},{96,144},{112,160... | collective-permute-start | bytes 12582920 | tf_op jit(solution)/shard_map/ppermute | solution.py:13
  587.9 0.7 copy-start
  588.7 6.1 collective-permute-start.1
  591.2 6.9 collective-permute-start.3
  591.2 7.9 %collective-permute-start.5 = (f32[512]{0:T(512)S(1)}, f32[512]{0:T(512)S(1)}, u32[]{:S(2)}, u32[]{:S(2)}) collective-permute-start(f32[512]{0:T(512)S(1)} %get-tuple-element.15), channel_id=1, source_target_pairs={{0,48},{16,64},{32,80},{48,96},{64,112},{80,128},{96,144},{112,160... | collective-permute-start | bytes 6152 | tf_op jit(solution)/shard_map/ppermute | solution.py:13
Sparse Core Ops, SparseCore 0:
  588.1 158.7 all-reduce.2
where the time goes:
time: 765 us; the launch traced here: 756 us
  waiting for transfers between devices  661 us (86%)
  matrix products  47.9 us (6%)
  between operations  19.5 us (3%)
  starting transfers between devices  13 us (2%)
  local copies, waits for them, and re-layouts  12.8 us (2%)
    ppermute x6, waiting for transfers between devices, shifted(): return lax.ppermute(value, axis, pairs)  513 us
    psum x1, waiting for transfers between devices, shards(): total = lax.psum(partial_tile, 'feat')  148 us
    dot_general x3, matrix products, shards(): lax.dot_general(visitor, grads, (((1,), (1,)), ((), ())), precision=lax.P...  47.9 us
  transfers between devices with their start and end apart: 7, of which 7 were waited for; matrix products, arithmetic and copies ran while one was open for 4% of the time, Pallas kernels for 0%

commit v1 on v0

v1 whole, which is shorter than its diff:
```python
import functools

import jax
import jax.numpy as jnp
from jax import lax
from jax.experimental import pallas as pl
from jax.experimental.pallas import tpu as pltpu
from jax.sharding import PartitionSpec as P

GROUP = 512
STEPS = 3
CHUNKS = 8
QUARTERS = 4
MESH = pl.DeviceIdType.MESH


def product(left, right):
    return lax.dot_general(
        left,
        right,
        (((1,), (1,)), ((), ())),
        precision=lax.Precision.HIGH,
        preferred_element_type=jnp.float32,
    )


def kernel(
    grads, near, mid, far, resid, out,
    near_v, mid_far_v, mid_v, far_v, far_far_v, res_v, res_far_v,
    part, parts_in, total, back_near, back_far,
    res_send, res_recv, relay_send, relay_recv, vis_send, vis_recv, cut_send, cut_recv,
    sum_send, sum_recv, ret_send, ret_recv, load_sem,
):
    n_ex, n_feat = lax.axis_size("ex"), lax.axis_size("feat")
    ex, feat = lax.axis_index("ex"), lax.axis_index("feat")
    rows = res_v.shape[1]
    wide = mid_v.shape[2]
    depth = grads.shape[1]
    narrow = depth - wide
    own = near.shape[1]
    quarter = own // QUARTERS
    owners = n_feat // QUARTERS

    def along(step):
        return {"ex": lax.rem(ex + step + n_ex, n_ex)}

    def across(step):
        return {"feat": lax.rem(feat + step, n_feat)}

    def remote(src, dst, send, recv, device):
        return pltpu.make_async_remote_copy(
            src_ref=src, dst_ref=dst, send_sem=send, recv_sem=recv, device_id=device, device_id_type=MESH
        )

    def residents(chunk):
        return remote(
            grads.at[pl.ds(pl.multiple_of(chunk * rows, rows), rows), :],
            res_v.at[chunk], res_send.at[chunk], res_recv.at[chunk], along(-1),
        )

    def relay(chunk):
        return remote(
            res_v.at[chunk, :, pl.ds(wide, narrow)],
            res_far_v.at[chunk], relay_send.at[chunk], relay_recv.at[chunk], along(-1),
        )

    def mid_visit(chunk):
        some = pl.ds(chunk * owners, owners)
        return remote(
            mid.at[some, :, pl.ds(0, wide)], mid_v.at[some], vis_send.at[chunk], vis_recv.at[chunk], along(1)
        )

    def far_cut_visit(chunk):
        some = pl.ds(chunk * owners, owners)
        return remote(
            far.at[some, :, pl.ds(wide, narrow)], far_far_v.at[some], cut_send.at[chunk], cut_recv.at[chunk], along(1)
        )

    def far_visit(chunk):
        q = chunk - QUARTERS
        return remote(
            far.at[:, pl.ds(pl.multiple_of(q * quarter, quarter), quarter), pl.ds(0, wide)],
            far_v.at[q], vis_send.at[chunk], vis_recv.at[chunk], along(2),
        )

    def start_visit(chunk):
        @pl.when(chunk < QUARTERS)
        def _():
            mid_visit(chunk).start()
            far_cut_visit(chunk).start()

        @pl.when(jnp.logical_and(chunk >= QUARTERS, chunk < 2 * QUARTERS))
        def _():
            far_visit(chunk).start()

    def columns(chunk):
        return pl.ds(pl.multiple_of(chunk * rows, rows), rows)

    def near_unit(c):
        return c, pl.ds(0, 1), pl.ds(0, own), columns(c), rows

    def mid_unit(c):
        return CHUNKS + c, pl.ds(1, 1), pl.ds(0, own), columns(c), rows

    def cut_unit(c):
        return 2 * CHUNKS + c, pl.ds(STEPS, 2), pl.ds(0, own), columns(c), rows

    last = (CHUNKS - 1) * rows
    upper = own - quarter
    far_units = (
        (3 * CHUNKS, pl.ds(2, 1), pl.ds(0, upper), pl.ds(0, last)),
        (3 * CHUNKS + 1, pl.ds(2, 1), pl.ds(upper, quarter), pl.ds(0, last)),
        (3 * CHUNKS + 2, pl.ds(2, 1), pl.ds(0, own), pl.ds(last, rows)),
    )

    def send_unit(unit):
        sem, tiles, lines, cols = unit[:4]

        @pl.loop(1, n_feat)
        def _(k):
            remote(
                part.at[lax.rem(feat + k, n_feat), tiles, lines, cols],
                parts_in.at[k - 1, tiles, lines, cols],
                sum_send.at[sem], sum_recv.at[sem], across(k),
            ).start()

    def all_parts(unit):
        sem, tiles, lines, cols = unit[:4]
        return remote(
            part.at[pl.ds(0, n_feat - 1), tiles, lines, cols],
            parts_in.at[:, tiles, lines, cols],
            sum_send.at[sem], sum_recv.at[sem], across(1),
        )

    def finish_unit(unit, far_home):
        _, tiles, lines, cols = unit[:4]
        all_parts(unit).wait_recv()
        value = part[feat, tiles, lines, cols]
        for k in range(n_feat - 1):
            value = value + parts_in[k, tiles, lines, cols]
        total[tiles, lines, cols] = value
        if far_home:
            remote(
                total.at[tiles, lines, cols], back_far.at[:, lines, cols], ret_send.at[1], ret_recv.at[1], along(2)
            ).start()
        else:
            remote(
                total.at[tiles, lines, cols], back_near.at[tiles, lines, cols], ret_send.at[0], ret_recv.at[0], along(1)
            ).start()

    barrier = pltpu.get_barrier_semaphore()
    for step in (-2, -1, 1, 2):
        pl.semaphore_signal(barrier, inc=1, device_id=along(step), device_id_type=MESH)

    @pl.loop(1, n_feat)
    def _(k):
        pl.semaphore_signal(barrier, inc=1, device_id=across(k), device_id_type=MESH)

    pl.semaphore_wait(barrier, 4 + n_feat - 1)

    for chunk in range(2):
        residents(chunk).start()
        mid_visit(chunk).start()
        far_cut_visit(chunk).start()
    loads = (
        pltpu.make_async_copy(near, near_v, load_sem.at[0]),
        pltpu.make_async_copy(mid.at[:, :, pl.ds(wide, narrow)], mid_far_v, load_sem.at[1]),
    )
    for load in loads:
        load.start()
    for load in loads:
        load.wait()

    def whole(ref):
        return ref[...].reshape(n_feat * own, ref.shape[2])

    def spread(value, height):
        return value.reshape(n_feat, height, rows)

    @pl.loop(0, CHUNKS)
    def _(t):
        residents(t).wait_recv()
        relay(t).start()
        residents(t).wait_send()

        @pl.when(t + 2 < CHUNKS)
        def _():
            residents(t + 2).start()

        part[:, 0, :, columns(t)] = spread(product(whole(near_v), res_v[t]), own)
        send_unit(near_unit(t))

        @pl.when(t < QUARTERS)
        def _():
            mid_visit(t).wait_recv()
            far_cut_visit(t).wait_recv()
            start_visit(t + 2)

        mid_first = jnp.where(t < QUARTERS - 1, t + 1, jnp.where(t == QUARTERS - 1, 0, t))

        @pl.loop(mid_first, t + 1)
        def _(c):
            part[:, 1, :, columns(c)] = spread(product(whole(mid_v), res_v[c, :, pl.ds(0, wide)]), own)
            send_unit(mid_unit(c))

        cut_first = jnp.where(t == QUARTERS, 0, t - 1)
        cut_end = jnp.where(t < QUARTERS, cut_first, jnp.where(t == CHUNKS - 1, CHUNKS, t))

        @pl.loop(cut_first, cut_end)
        def _(c):
            relay(c).wait_recv()
            block = res_far_v[c]
            part[:, STEPS, :, columns(c)] = spread(product(whole(mid_far_v), block), own)
            part[:, STEPS + 1, :, columns(c)] = spread(product(whole(far_far_v), block), own)
            send_unit(cut_unit(c))

        @pl.when(t > 0)
        def _():
            finish_unit(near_unit(t - 1), False)

        done_first = jnp.where(t == QUARTERS, 0, t - 1)
        done_end = jnp.where(t < QUARTERS, done_first, t)

        @pl.loop(done_first, done_end)
        def _(c):
            finish_unit(mid_unit(c), False)

        cut_done_first = jnp.where(t == QUARTERS + 1, 0, t - 2)
        cut_done_end = jnp.where(t < QUARTERS + 1, cut_done_first, t - 1)

        @pl.loop(cut_done_first, cut_done_end)
        def _(c):
            finish_unit(cut_unit(c), True)

        @pl.when(t >= QUARTERS)
        def _():
            far_visit(t).wait_recv()
            start_visit(t + 2)
            q = t - QUARTERS

            def piece(q, c):
                lines = pl.ds(pl.multiple_of(q * quarter, quarter), quarter)
                value = product(
                    far_v[q].reshape(n_feat * quarter, wide), res_v[c, :, pl.ds(0, wide)]
                )
                part[:, 2, lines, columns(c)] = spread(value, quarter)

            @pl.loop(0, t + q + 1)
            def _(i):
                earlier = i < t
                piece(jnp.where(earlier, q, i - t), jnp.where(earlier, i, t))

            @pl.when(t == CHUNKS - 2)
            def _():
                send_unit(far_units[0])

            @pl.when(t == CHUNKS - 1)
            def _():
                send_unit(far_units[1])
                send_unit(far_units[2])

    finish_unit(near_unit(CHUNKS - 1), False)
    finish_unit(mid_unit(CHUNKS - 1), False)
    for c in (CHUNKS - 2, CHUNKS - 1):
        finish_unit(cut_unit(c), True)
    for unit in far_units:
        finish_unit(unit, False)

    remote(total.at[pl.ds(0, STEPS)], back_near, ret_send.at[0], ret_recv.at[0], along(1)).wait()
    remote(total.at[pl.ds(STEPS, 2)], back_far, ret_send.at[1], ret_recv.at[1], along(2)).wait()
    weight = resid[...]
    dots = back_near[0]
    out[0] = dots * dots * weight
    for step in (1, 2):
        dots = back_near[step] + back_far[step - 1]
        out[step] = dots * dots * weight

    @pl.loop(0, CHUNKS)
    def _(t):
        relay(t).wait_send()
        all_parts(near_unit(t)).wait_send()
        all_parts(mid_unit(t)).wait_send()
        all_parts(cut_unit(t)).wait_send()

    for unit in far_units:
        all_parts(unit).wait_send()

    @pl.loop(0, QUARTERS)
    def _(t):
        mid_visit(t).wait_send()
        far_cut_visit(t).wait_send()
        far_visit(t + QUARTERS).wait_send()


def shards(grads, resid, offsets):
    n_feat = lax.axis_size("feat")
    count, depth = grads.shape
    own = GROUP // n_feat
    rows = count // CHUNKS
    narrow = depth // 4
    wide = depth - narrow
    scale = jnp.sqrt(resid)
    blocks = []
    for step in range(STEPS):
        start = offsets[step]
        block = lax.dynamic_slice_in_dim(grads, start, GROUP, 0)
        block_scale = lax.dynamic_slice_in_dim(scale, start, GROUP, 0)
        blocks.append((block * block_scale[:, None]).reshape(n_feat, own, depth))
    f32 = jnp.float32
    units = 3 * CHUNKS + 3
    dma = pltpu.SemaphoreType.DMA
    return pl.pallas_call(
        kernel,
        out_shape=jax.ShapeDtypeStruct((STEPS, own, count), f32),
        in_specs=[pl.BlockSpec(memory_space=pl.ANY)] * 4 + [pl.BlockSpec(memory_space=pltpu.VMEM)],
        out_specs=pl.BlockSpec(memory_space=pltpu.VMEM),
        scratch_shapes=[
            pltpu.VMEM((n_feat, own, depth), f32),
            pltpu.VMEM((n_feat, own, narrow), f32),
            pltpu.VMEM((n_feat, own, wide), f32),
            pltpu.VMEM((QUARTERS, n_feat, own // QUARTERS, wide), f32),
            pltpu.VMEM((n_feat, own, narrow), f32),
            pltpu.VMEM((CHUNKS, rows, depth), f32),
            pltpu.VMEM((CHUNKS, rows, narrow), f32),
            pltpu.VMEM((n_feat, STEPS + 2, own, count), f32),
            pltpu.VMEM((n_feat - 1, STEPS + 2, own, count), f32),
            pltpu.VMEM((STEPS + 2, own, count), f32),
            pltpu.VMEM((STEPS, own, count), f32),
            pltpu.VMEM((2, own, count), f32),
            dma((CHUNKS,)), dma((CHUNKS,)), dma((CHUNKS,)), dma((CHUNKS,)),
            dma((CHUNKS,)), dma((CHUNKS,)), dma((QUARTERS,)), dma((QUARTERS,)),
            dma((units,)), dma((units,)), dma((2,)), dma((2,)), dma((2,)),
        ],
        compiler_params=pltpu.CompilerParams(
            collective_id=0, has_side_effects=True, vmem_limit_bytes=60 * 2**20
        ),
    )(grads, *blocks, resid[None, :])


def solution(mesh):
    return jax.shard_map(
        shards,
        mesh=mesh,
        in_specs=(P("ex", "feat"), P("ex"), P()),
        out_specs=P(None, "feat", "ex"),
        check_vma=False,
    )
```

time: 765 us -> 430 us (0.56)
  the two profiles are of different devices: /device:TPU:1 before, /device:TPU:72 now
where the time goes in v1:
time: 430 us; the launch traced here: 429 us
  Pallas kernels  409 us (95%)
  other arithmetic  10.7 us (2%)
  between operations  5.67 us (1%)
    pallas_call x1, Pallas kernels, shards(): pl.pallas_call(kernel, out_shape=jax.ShapeDtypeStruct((STEPS, own, count)...  409 us
    mul x1, other arithmetic, shards(): blocks.append((block * block_scale[:, None]).reshape(n_feat, own, depth))  10.7 us

profile of v1, /device:TPU:72, one launch (start us, length us, event | category | flops | bytes accessed | tf_op | source)
XLA Modules:
  0.0 429.3 jit_solution(12545757019453535956)
XLA Ops:
  0.0 1.4 fusion.1
  7.0 0.7 sqrt.3
  7.7 0.1 fusion
  7.8 10.7 %dynamic-slice_multiply_fusion = (f32[512,2048]{1,0:T(8,128)}, f32[512,2048]{1,0:T(8,128)}, f32[512,2048]{1,0:T(8,128)}) fusion(f32[1024,2048]{1,0:T(8,128)} %grads.1, s32[]{:T(128)S(6)} %select_n.14, f32[512]{0:T(512)S(1)} %get-tuple-element.8, f32[512]{0:T(512)S(1)} %get-tuple-element.9, s32[]{:T(128)S(6)} %select_n.13, f32[512]{0:T(512)S(1)} %get-tuple-element.10, ...), kind=kLoop, calls=%fused_computation | loop fusion | flops 3145728 | bytes 25171980 | tf_op jit(solution)/shard_map/mul | solution.py:308
  18.6 409.0 %shard_map.37 = f32[3,32,1024]{2,1,0:T(8,128)} custom-call(f32[1024,2048]{1,0:T(8,128)} %grads.1, f32[16,32,2048]{2,1,0:T(8,128)} %bitcast.9, f32[16,32,2048]{2,1,0:T(8,128)} %bitcast.8, f32[16,32,2048]{2,1,0:T(8,128)} %bitcast.7, f32[1,1024]{1,0:T(1,128)} %bitcast.10), custom_call_target="tpu_custom_call" | custom-call | tf_op jit(solution)/shard_map/pallas_call | solution.py:312
  427.6 1.8 copy.5

commit v2 on v1

v2 whole, which is shorter than its diff:
```python
import functools

import jax
import jax.numpy as jnp
from jax import lax
from jax.experimental import pallas as pl
from jax.experimental.pallas import tpu as pltpu
from jax.sharding import PartitionSpec as P

GROUP = 512
STEPS = 3
CHUNKS = 8
AHEAD = 3
QUARTERS = 4
HALF = CHUNKS // 2
MESH = pl.DeviceIdType.MESH


def product(left, right):
    return lax.dot_general(
        left,
        right,
        (((1,), (1,)), ((), ())),
        precision=lax.Precision.HIGH,
        preferred_element_type=jnp.float32,
    )


def kernel(
    grads, near, mid, far, resid, out,
    near_v, mid_far_v, mid_v, far_v, far_far_v, res_v, res_far_v,
    part, core_in, row_in, pair_in, total, back_near, back_far,
    far_part, far_core_in, far_row_in, far_pair_in, far_total, far_back,
    res_send, res_recv, relay_send, relay_recv, vis_send, vis_recv, cut_send, cut_recv,
    core_send, core_recv, row_send, row_recv, pair_send, pair_recv, ret_send, ret_recv, load_sem,
):
    n_ex, n_feat = lax.axis_size("ex"), lax.axis_size("feat")
    ex, feat = lax.axis_index("ex"), lax.axis_index("feat")
    rows = res_v.shape[1]
    wide = mid_v.shape[2]
    depth = grads.shape[1]
    narrow = depth - wide
    own = near.shape[1]
    quarter = own // QUARTERS
    owners = n_feat // QUARTERS
    n_row = n_feat // 4
    row, pair, core = feat // 4, lax.rem(feat // 2, 2), lax.rem(feat, 2)

    def along(step):
        return {"ex": lax.rem(ex + step + n_ex, n_ex)}

    def other_core():
        return {"feat": feat + 1 - 2 * core}

    def in_row(step):
        return {"feat": lax.rem(row + step, n_row) * 4 + lax.rem(feat, 4)}

    def other_pair():
        return {"feat": feat + 2 - 4 * pair}

    def remote(src, dst, send, recv, device):
        return pltpu.make_async_remote_copy(
            src_ref=src, dst_ref=dst, send_sem=send, recv_sem=recv, device_id=device, device_id_type=MESH
        )

    def residents(chunk):
        return remote(
            grads.at[pl.ds(pl.multiple_of(chunk * rows, rows), rows), :],
            res_v.at[chunk], res_send.at[chunk], res_recv.at[chunk], along(-1),
        )

    def relay(chunk):
        return remote(
            res_v.at[chunk, :, pl.ds(wide, narrow)],
            res_far_v.at[chunk], relay_send.at[chunk], relay_recv.at[chunk], along(-1),
        )

    def mid_visit(chunk):
        some = pl.ds(chunk * owners, owners)
        return remote(
            mid.at[some, :, pl.ds(0, wide)], mid_v.at[some], vis_send.at[chunk], vis_recv.at[chunk], along(1)
        )

    def far_cut_visit(chunk):
        some = pl.ds(chunk * owners, owners)
        return remote(
            far.at[some, :, pl.ds(wide, narrow)], far_far_v.at[some], cut_send.at[chunk], cut_recv.at[chunk], along(1)
        )

    def far_visit(chunk):
        q = chunk - QUARTERS
        return remote(
            far.at[:, pl.ds(pl.multiple_of(q * quarter, quarter), quarter), pl.ds(0, wide)],
            far_v.at[q], vis_send.at[chunk], vis_recv.at[chunk], along(2),
        )

    def start_visit(chunk):
        @pl.when(chunk < QUARTERS)
        def _():
            mid_visit(chunk).start()
            far_cut_visit(chunk).start()

        @pl.when(jnp.logical_and(chunk >= QUARTERS, chunk < 2 * QUARTERS))
        def _():
            far_visit(chunk).start()

    def near_unit(c):
        return c, False, pl.ds(0, 1), pl.ds(c, 1)

    def whole_unit(c):
        return c, False, pl.ds(0, 4), pl.ds(c, 1)

    first_unit = (CHUNKS, False, pl.ds(1, 3), pl.ds(0, HALF))
    far_units = (
        (CHUNKS + 1, True, pl.ds(0, QUARTERS - 1), pl.ds(0, CHUNKS - 1)),
        (CHUNKS + 2, True, pl.ds(0, QUARTERS - 1), pl.ds(CHUNKS - 1, 1)),
        (CHUNKS + 3, True, pl.ds(QUARTERS - 1, 1), pl.ds(0, CHUNKS)),
    )

    def own_part(unit, c, x, y):
        _, far, i, j = unit
        return (far_part, (c, x, y, i, j)) if far else (part, (c, i, j, x, y))

    def from_core(unit, x):
        _, far, i, j = unit
        return (far_core_in, (x, slice(None), i, j)) if far else (core_in, (i, j, x))

    def from_row(unit, k):
        _, far, i, j = unit
        return (far_row_in, (k, slice(None), i, j)) if far else (row_in, (k, i, j))

    def from_pair(unit):
        _, far, i, j = unit
        return (far_pair_in, (i, j)) if far else (pair_in, (i, j))

    def at(place):
        return place[0].at[place[1]]

    def read(place):
        return place[0][place[1]]

    every = slice(None)

    def core_copy(unit):
        sem = unit[0]
        return remote(
            at(own_part(unit, 1 - core, every, every)), at(from_core(unit, every)),
            core_send.at[sem], core_recv.at[sem], other_core(),
        )

    def row_copy(unit, step):
        sem = unit[0]
        return remote(
            at(own_part(unit, core, lax.rem(row + step, n_row), every)), at(from_row(unit, step - 1)),
            row_send.at[sem], row_recv.at[sem], in_row(step),
        )

    def row_copies(unit):
        sem = unit[0]
        block = at(from_row(unit, every))
        return remote(block, block, row_send.at[sem], row_recv.at[sem], in_row(1))

    def pair_copy(unit):
        sem = unit[0]
        return remote(
            at(own_part(unit, core, row, 1 - pair)), at(from_pair(unit)),
            pair_send.at[sem], pair_recv.at[sem], other_pair(),
        )

    def start_sum(unit):
        core_copy(unit).start()

    def sum_cores(unit):
        core_copy(unit).wait_recv()

        @pl.loop(0, n_row)
        def _(x):
            ref, index = own_part(unit, core, x, every)
            ref[index] = ref[index] + read(from_core(unit, x))

        for step in range(1, n_row):
            row_copy(unit, step).start()

    def sum_row(unit):
        row_copies(unit).wait_recv()
        ref, index = own_part(unit, core, row, every)
        value = ref[index]
        for k in range(n_row - 1):
            value = value + read(from_row(unit, k))
        ref[index] = value
        pair_copy(unit).start()

    def send_back(src, dst, sem, step):
        remote(src, dst, ret_send.at[sem], ret_recv.at[sem], along(step)).start()

    def sum_pair(unit):
        pair_copy(unit).wait_recv()
        _, far, i, j = unit
        value = read(own_part(unit, core, row, pair)) + read(from_pair(unit))
        if far:
            far_total[i, j] = value
            send_back(far_total.at[i, j], far_back.at[i, j], 2, 1)
            return
        total[i, j] = value
        low, high = i.start, i.start + i.size
        near_home = pl.ds(low, min(high, 2) - low)
        send_back(total.at[near_home, j], back_near.at[near_home, j], 0, 1)
        if high > 2:
            send_back(total.at[pl.ds(2, 2), j], back_far.at[:, j], 1, 2)

    def wait_sum(unit):
        core_copy(unit).wait_send()
        row_copies(unit).wait_send()
        pair_copy(unit).wait_send()

    def advance(ready, stage):
        @pl.when(jnp.logical_and(ready >= 0, ready < HALF))
        def _():
            stage(near_unit(ready))

        @pl.when(ready == HALF - 1)
        def _():
            stage(first_unit)

        @pl.when(jnp.logical_and(ready >= HALF, ready < CHUNKS - 1))
        def _():
            stage(whole_unit(ready))

        @pl.when(ready == CHUNKS - 2)
        def _():
            stage(far_units[0])

    barrier = pltpu.get_barrier_semaphore()
    for step in (-2, -1, 1, 2):
        pl.semaphore_signal(barrier, inc=1, device_id=along(step), device_id_type=MESH)

    for device in (other_core(), other_pair()) + tuple(in_row(step) for step in range(1, n_row)):
        pl.semaphore_signal(barrier, inc=1, device_id=device, device_id_type=MESH)
    pl.semaphore_wait(barrier, 4 + 2 + n_row - 1)

    for chunk in range(AHEAD):
        residents(chunk).start()
        mid_visit(chunk).start()
        far_cut_visit(chunk).start()
    loads = (
        pltpu.make_async_copy(near, near_v, load_sem.at[0]),
        pltpu.make_async_copy(mid.at[:, :, pl.ds(wide, narrow)], mid_far_v, load_sem.at[1]),
    )
    for load in loads:
        load.start()
    for load in loads:
        load.wait()

    def whole(ref):
        return ref[...].reshape(n_feat * own, ref.shape[2])

    def keep(value, tile, c):
        value = value.reshape(n_row, 2, 2, own, rows)
        for k in range(2):
            part[k, tile, c] = value[:, :, k]

    def near_tile(c):
        keep(product(whole(near_v), res_v[c]), 0, c)

    def mid_tile(c):
        keep(product(whole(mid_v), res_v[c, :, pl.ds(0, wide)]), 1, c)

    def cut_tiles(c):
        relay(c).wait_recv()
        block = res_far_v[c]
        keep(product(whole(mid_far_v), block), 2, c)
        keep(product(whole(far_far_v), block), 3, c)

    def far_tile(q, c):
        value = product(far_v[q].reshape(n_feat * quarter, wide), res_v[c, :, pl.ds(0, wide)])
        value = value.reshape(n_row, 2, 2, quarter, rows)
        for k in range(2):
            far_part[k, :, :, q, c] = value[:, :, k]

    @pl.loop(0, CHUNKS - 1)
    def _(t):
        residents(t).wait_recv()
        relay(t).start()
        residents(t).wait_send()

        @pl.when(t + AHEAD < CHUNKS)
        def _():
            residents(t + AHEAD).start()

        near_tile(t)

        @pl.when(t < QUARTERS)
        def _():
            mid_visit(t).wait_recv()
            far_cut_visit(t).wait_recv()
            start_visit(t + AHEAD)

        @pl.loop(jnp.where(t < HALF - 1, t + 1, jnp.where(t == HALF - 1, 0, t)), t + 1)
        def _(c):
            mid_tile(c)

        @pl.when(t >= QUARTERS)
        def _():
            far_visit(t).wait_recv()
            start_visit(t + AHEAD)
            q = t - QUARTERS

            @pl.loop(0, t + q + 1)
            def _(i):
                earlier = i < t
                far_tile(jnp.where(earlier, q, i - t), jnp.where(earlier, i, t))

        @pl.loop(jnp.where(t < HALF - 1, t + 1, jnp.where(t == HALF - 1, 0, t)), t + 1)
        def _(c):
            cut_tiles(c)

        advance(t, start_sum)
        advance(t - 2, sum_row)
        advance(t - 1, sum_cores)

    end = CHUNKS - 1
    residents(end).wait_recv()
    relay(end).start()
    residents(end).wait_send()
    near_tile(end)
    mid_tile(end)
    advance(jnp.int32(end - 1), sum_cores)
    advance(jnp.int32(end - 2), sum_row)
    for q in range(QUARTERS - 1):
        far_tile(q, end)
    start_sum(far_units[1])
    cut_tiles(end)
    start_sum(whole_unit(end))
    advance(jnp.int32(end - 1), sum_row)
    for stage in (sum_cores, sum_row):
        stage(far_units[1])
        stage(whole_unit(end))

    @pl.loop(0, end)
    def _(ready):
        advance(ready, sum_pair)

    for unit in (far_units[1], whole_unit(end)):
        sum_pair(unit)
    far_visit(end).wait_recv()

    @pl.loop(0, CHUNKS)
    def _(c):
        far_tile(QUARTERS - 1, c)

    start_sum(far_units[2])
    for stage in (sum_cores, sum_row, sum_pair):
        stage(far_units[2])

    remote(total.at[pl.ds(0, 2)], back_near, ret_send.at[0], ret_recv.at[0], along(1)).wait()
    remote(total.at[pl.ds(2, 2)], back_far, ret_send.at[1], ret_recv.at[1], along(2)).wait()
    remote(far_total, far_back, ret_send.at[2], ret_recv.at[2], along(1)).wait()
    for c in range(CHUNKS):
        cols = pl.ds(c * rows, rows)
        weight = resid[:, cols]
        tiles = (
            back_near[0, c],
            back_near[1, c] + back_far[0, c],
            far_back[:, c].reshape(own, rows) + back_far[1, c],
        )
        for step, dots in enumerate(tiles):
            out[step, :, cols] = dots * dots * weight

    @pl.loop(0, CHUNKS)
    def _(t):
        relay(t).wait_send()

        @pl.when(t < HALF)
        def _():
            wait_sum(near_unit(t))

        @pl.when(t >= HALF)
        def _():
            wait_sum(whole_unit(t))

    for unit in (first_unit,) + far_units:
        wait_sum(unit)

    @pl.loop(0, QUARTERS)
    def _(t):
        mid_visit(t).wait_send()
        far_cut_visit(t).wait_send()
        far_visit(t + QUARTERS).wait_send()


def shards(grads, resid, offsets):
    n_feat = lax.axis_size("feat")
    count, depth = grads.shape
    own = GROUP // n_feat
    rows = count // CHUNKS
    narrow = depth // 4
    wide = depth - narrow
    scale = jnp.sqrt(resid)
    blocks = []
    for step in range(STEPS):
        start = offsets[step]
        block = lax.dynamic_slice_in_dim(grads, start, GROUP, 0)
        block_scale = lax.dynamic_slice_in_dim(scale, start, GROUP, 0)
        blocks.append((block * block_scale[:, None]).reshape(n_feat, own, depth))
    f32 = jnp.float32
    units = CHUNKS + 4
    dma = pltpu.SemaphoreType.DMA
    xs = n_feat // 4
    far = (QUARTERS, CHUNKS, own // QUARTERS, rows)
    return pl.pallas_call(
        kernel,
        out_shape=jax.ShapeDtypeStruct((STEPS, own, count), f32),
        in_specs=[pl.BlockSpec(memory_space=pl.ANY)] * 4 + [pl.BlockSpec(memory_space=pltpu.VMEM)],
        out_specs=pl.BlockSpec(memory_space=pltpu.VMEM),
        scratch_shapes=[
            pltpu.VMEM((n_feat, own, depth), f32),
            pltpu.VMEM((n_feat, own, narrow), f32),
            pltpu.VMEM((n_feat, own, wide), f32),
            pltpu.VMEM((QUARTERS, n_feat, own // QUARTERS, wide), f32),
            pltpu.VMEM((n_feat, own, narrow), f32),
            pltpu.VMEM((CHUNKS, rows, depth), f32),
            pltpu.VMEM((CHUNKS, rows, narrow), f32),
            pltpu.VMEM((2, 4, CHUNKS, xs, 2, own, rows), f32),
            pltpu.VMEM((4, CHUNKS, xs, 2, own, rows), f32),
            pltpu.VMEM((xs - 1, 4, CHUNKS, 2, own, rows), f32),
            pltpu.VMEM((4, CHUNKS, own, rows), f32),
            pltpu.VMEM((4, CHUNKS, own, rows), f32),
            pltpu.VMEM((2, CHUNKS, own, rows), f32),
            pltpu.VMEM((2, CHUNKS, own, rows), f32),
            pltpu.VMEM((2, xs, 2) + far, f32),
            pltpu.VMEM((xs, 2) + far, f32),
            pltpu.VMEM((xs - 1, 2) + far, f32),
            pltpu.VMEM(far, f32),
            pltpu.VMEM(far, f32),
            pltpu.VMEM(far, f32),
            dma((CHUNKS,)), dma((CHUNKS,)), dma((CHUNKS,)), dma((CHUNKS,)),
            dma((CHUNKS,)), dma((CHUNKS,)), dma((QUARTERS,)), dma((QUARTERS,)),
            dma((units,)), dma((units,)), dma((units,)), dma((units,)), dma((units,)), dma((units,)), dma((3,)), dma((3,)), dma((2,)),
        ],
        compiler_params=pltpu.CompilerParams(
            collective_id=0, has_side_effects=True, vmem_limit_bytes=60 * 2**20
        ),
    )(grads, *blocks, resid[None, :])


def solution(mesh):
    return jax.shard_map(
        shards,
        mesh=mesh,
        in_specs=(P("ex", "feat"), P("ex"), P()),
        out_specs=P(None, "feat", "ex"),
        check_vma=False,
    )
```

time: 430 us -> 309 us (0.72)
  the two profiles are of different devices: /device:TPU:72 before, /device:TPU:1 now
where the time goes in v2:
time: 309 us
  Pallas kernels  289 us (94%)
  other arithmetic  10.5 us (3%)
  between operations  5.67 us (2%)
  local copies, waits for them, and re-layouts  3.92 us (1%)
    pallas_call x1, Pallas kernels, shards(): pl.pallas_call(kernel, out_shape=jax.ShapeDtypeStruct((STEPS, own, count)...  289 us
    mul x1, other arithmetic, shards(): blocks.append((block * block_scale[:, None]).reshape(n_feat, own, depth))  10.5 us

profile of v2, /device:TPU:1, one launch (start us, length us, event | category | flops | bytes accessed | tf_op | source)
XLA Modules:
  0.0 309.0 jit_solution(8738310328400676509)
XLA Ops:
  0.0 1.4 fusion.1
  7.0 0.7 sqrt.3
  7.7 0.1 fusion
  7.8 10.5 %dynamic-slice_multiply_fusion = (f32[512,2048]{1,0:T(8,128)}, f32[512,2048]{1,0:T(8,128)}, f32[512,2048]{1,0:T(8,128)}) fusion(f32[1024,2048]{1,0:T(8,128)} %grads.1, s32[]{:T(128)S(6)} %select_n.14, f32[512]{0:T(512)S(1)} %get-tuple-element.8, f32[512]{0:T(512)S(1)} %get-tuple-element.9, s32[]{:T(128)S(6)} %select_n.13, f32[512]{0:T(512)S(1)} %get-tuple-element.10, ...), kind=kLoop, calls=%fused_computation | loop fusion | flops 3145728 | bytes 25171980 | tf_op jit(solution)/shard_map/mul | solution.py:404
  18.3 288.9 %shard_map.37 = f32[3,32,1024]{2,1,0:T(8,128)} custom-call(f32[1024,2048]{1,0:T(8,128)} %grads.1, f32[16,32,2048]{2,1,0:T(8,128)} %bitcast.9, f32[16,32,2048]{2,1,0:T(8,128)} %bitcast.8, f32[16,32,2048]{2,1,0:T(8,128)} %bitcast.7, f32[1,1024]{1,0:T(1,128)} %bitcast.10), custom_call_target="tpu_custom_call" | custom-call | tf_op jit(solution)/shard_map/pallas_call | solution.py:410
  307.2 1.8 copy.5

commit v3 on v2

--- a/solution.py
+++ b/solution.py
@@ -10,9 +10,10 @@
 GROUP = 512
 STEPS = 3
 CHUNKS = 8
-AHEAD = 3
+AHEAD = 2
 QUARTERS = 4
 HALF = CHUNKS // 2
+PICKED = 512
 MESH = pl.DeviceIdType.MESH
 
 
@@ -27,8 +28,8 @@
 
 
 def kernel(
-    grads, near, mid, far, resid, out,
-    near_v, mid_far_v, mid_v, far_v, far_far_v, res_v, res_far_v,
+    offsets, grads, resid, out,
+    grads_v, near_v, mid, far, mid_v, far_v, far_far_v, res_v, res_far_v,
     part, core_in, row_in, pair_in, total, back_near, back_far,
     far_part, far_core_in, far_row_in, far_pair_in, far_total, far_back,
     res_send, res_recv, relay_send, relay_recv, vis_send, vis_recv, cut_send, cut_recv,
@@ -40,7 +41,7 @@
     wide = mid_v.shape[2]
     depth = grads.shape[1]
     narrow = depth - wide
-    own = near.shape[1]
+    own = near_v.shape[1]
     quarter = own // QUARTERS
     owners = n_feat // QUARTERS
     n_row = n_feat // 4
@@ -240,16 +241,40 @@
 
     for chunk in range(AHEAD):
         residents(chunk).start()
+    load = pltpu.make_async_copy(grads, grads_v, load_sem)
+    load.start()
+    load.wait()
+
+    count = grads_v.shape[0]
+    some_rows = owners * own
+
+    def take(step, block, chunk):
+        line = lax.broadcasted_iota(jnp.int32, (some_rows, count), 0) + (offsets[step] + chunk * some_rows)
+        source = lax.broadcasted_iota(jnp.int32, (some_rows, count), 1)
+        pick = jnp.where(line == source, jnp.sqrt(resid[...]), 0.0)
+
+        @pl.loop(0, depth // PICKED)
+        def _(i):
+            cols = pl.ds(pl.multiple_of(i * PICKED, PICKED), PICKED)
+            value = lax.dot_general(
+                pick,
+                grads_v[:, cols],
+                (((1,), (0,)), ((), ())),
+                precision=lax.Precision.HIGH,
+                preferred_element_type=jnp.float32,
+            )
+            block[pl.ds(chunk * owners, owners), :, cols] = value.reshape(owners, own, PICKED)
+
+    @pl.loop(0, AHEAD)
+    def _(chunk):
+        take(1, mid, chunk)
+        take(2, far, chunk)
         mid_visit(chunk).start()
         far_cut_visit(chunk).start()
-    loads = (
-        pltpu.make_async_copy(near, near_v, load_sem.at[0]),
-        pltpu.make_async_copy(mid.at[:, :, pl.ds(wide, narrow)], mid_far_v, load_sem.at[1]),
-    )
-    for load in loads:
-        load.start()
-    for load in loads:
-        load.wait()
+
+    @pl.loop(0, QUARTERS)
+    def _(chunk):
+        take(0, near_v, chunk)
 
     def whole(ref):
         return ref[...].reshape(n_feat * own, ref.shape[2])
@@ -268,7 +293,7 @@
     def cut_tiles(c):
         relay(c).wait_recv()
         block = res_far_v[c]
-        keep(product(whole(mid_far_v), block), 2, c)
+        keep(product(mid[:, :, pl.ds(wide, narrow)].reshape(n_feat * own, narrow), block), 2, c)
         keep(product(whole(far_far_v), block), 3, c)
 
     def far_tile(q, c):
@@ -293,6 +318,12 @@
         def _():
             mid_visit(t).wait_recv()
             far_cut_visit(t).wait_recv()
+
+            @pl.when(t + AHEAD < QUARTERS)
+            def _():
+                take(1, mid, t + AHEAD)
+                take(2, far, t + AHEAD)
+
             start_visit(t + AHEAD)
 
         @pl.loop(jnp.where(t < HALF - 1, t + 1, jnp.where(t == HALF - 1, 0, t)), t + 1)
@@ -326,6 +357,11 @@
     mid_tile(end)
     advance(jnp.int32(end - 1), sum_cores)
     advance(jnp.int32(end - 2), sum_row)
+
+    @pl.loop(0, end - 2)
+    def _(ready):
+        advance(ready, sum_pair)
+
     for q in range(QUARTERS - 1):
         far_tile(q, end)
     start_sum(far_units[1])
@@ -336,7 +372,7 @@
         stage(far_units[1])
         stage(whole_unit(end))
 
-    @pl.loop(0, end)
+    @pl.loop(end - 2, end)
     def _(ready):
         advance(ready, sum_pair)
 
@@ -395,13 +431,6 @@
     rows = count // CHUNKS
     narrow = depth // 4
     wide = depth - narrow
-    scale = jnp.sqrt(resid)
-    blocks = []
-    for step in range(STEPS):
-        start = offsets[step]
-        block = lax.dynamic_slice_in_dim(grads, start, GROUP, 0)
-        block_scale = lax.dynamic_slice_in_dim(scale, start, GROUP, 0)
-        blocks.append((block * block_scale[:, None]).reshape(n_feat, own, depth))
     f32 = jnp.float32
     units = CHUNKS + 4
     dma = pltpu.SemaphoreType.DMA
@@ -410,11 +439,17 @@
     return pl.pallas_call(
         kernel,
         out_shape=jax.ShapeDtypeStruct((STEPS, own, count), f32),
-        in_specs=[pl.BlockSpec(memory_space=pl.ANY)] * 4 + [pl.BlockSpec(memory_space=pltpu.VMEM)],
+        in_specs=[
+            pl.BlockSpec(memory_space=pltpu.SMEM),
+            pl.BlockSpec(memory_space=pl.ANY),
+            pl.BlockSpec(memory_space=pltpu.VMEM),
+        ],
         out_specs=pl.BlockSpec(memory_space=pltpu.VMEM),
         scratch_shapes=[
+            pltpu.VMEM((count, depth), f32),
             pltpu.VMEM((n_feat, own, depth), f32),
-            pltpu.VMEM((n_feat, own, narrow), f32),
+            pltpu.VMEM((n_feat, own, depth), f32),
+            pltpu.VMEM((n_feat, own, depth), f32),
             pltpu.VMEM((n_feat, own, wide), f32),
             pltpu.VMEM((QUARTERS, n_feat, own // QUARTERS, wide), f32),
             pltpu.VMEM((n_feat, own, narrow), f32),
@@ -435,12 +470,12 @@
             pltpu.VMEM(far, f32),
             dma((CHUNKS,)), dma((CHUNKS,)), dma((CHUNKS,)), dma((CHUNKS,)),
             dma((CHUNKS,)), dma((CHUNKS,)), dma((QUARTERS,)), dma((QUARTERS,)),
-            dma((units,)), dma((units,)), dma((units,)), dma((units,)), dma((units,)), dma((units,)), dma((3,)), dma((3,)), dma((2,)),
+            dma((units,)), dma((units,)), dma((units,)), dma((units,)), dma((units,)), dma((units,)), dma((3,)), dma((3,)), dma,
         ],
         compiler_params=pltpu.CompilerParams(
-            collective_id=0, has_side_effects=True, vmem_limit_bytes=60 * 2**20
+            collective_id=0, has_side_effects=True, vmem_limit_bytes=62 * 2**20
         ),
-    )(grads, *blocks, resid[None, :])
+    )(offsets, grads, resid[None, :])
 
 
 def solution(mesh):

time: 309 us -> 287 us (0.929)
  other arithmetic: 10.5 us -> 0 us
  between operations: 5.67 us -> 0.01 us
  Pallas kernels: 289 us -> 285 us
    mul x1 -> x0, other arithmetic: 10.5 us -> none  [shards(): blocks.append((block * block_scale[:, None]).reshape(n_feat, own, depth))]
    pallas_call x1, Pallas kernels: 289 us -> 285 us  [shards(): pl.pallas_call(kernel, out_shape=jax.ShapeDtypeStruct((STEPS, own, count)...]
where the time goes in v3:
time: 287 us
  Pallas kernels  285 us (99%)
    pallas_call x1, Pallas kernels, shards(): pl.pallas_call(kernel, out_shape=jax.ShapeDtypeStruct((STEPS, own, count)...  285 us

profile of v3, /device:TPU:1, one launch (start us, length us, event | category | flops | bytes accessed | tf_op | source)
XLA Modules:
  0.0 286.7 jit_solution(1531642146935973487)
XLA Ops:
  0.0 284.9 %shard_map.37 = f32[3,32,1024]{2,1,0:T(8,128)} custom-call(s32[3]{0:T(128)} %offsets.1, f32[1024,2048]{1,0:T(8,128)} %grads.1, f32[1,1024]{1,0:T(1,128)} %bitcast.1), custom_call_target="tpu_custom_call" | custom-call | tf_op jit(solution)/shard_map/pallas_call | solution.py:439
  284.9 1.8 copy.5

commit v4 on v3

--- a/solution.py
+++ b/solution.py
@@ -115,7 +115,8 @@
     far_units = (
         (CHUNKS + 1, True, pl.ds(0, QUARTERS - 1), pl.ds(0, CHUNKS - 1)),
         (CHUNKS + 2, True, pl.ds(0, QUARTERS - 1), pl.ds(CHUNKS - 1, 1)),
-        (CHUNKS + 3, True, pl.ds(QUARTERS - 1, 1), pl.ds(0, CHUNKS)),
+        (CHUNKS + 3, True, pl.ds(QUARTERS - 1, 1), pl.ds(0, HALF)),
+        (CHUNKS + 4, True, pl.ds(QUARTERS - 1, 1), pl.ds(HALF, HALF)),
     )
 
     def own_part(unit, c, x, y):
@@ -380,13 +381,17 @@
         sum_pair(unit)
     far_visit(end).wait_recv()
 
-    @pl.loop(0, CHUNKS)
-    def _(c):
-        far_tile(QUARTERS - 1, c)
-
-    start_sum(far_units[2])
+    for half in range(2):
+
+        @pl.loop(half * HALF, (half + 1) * HALF)
+        def _(c):
+            far_tile(QUARTERS - 1, c)
+
+        start_sum(far_units[2 + half])
+
     for stage in (sum_cores, sum_row, sum_pair):
-        stage(far_units[2])
+        for unit in far_units[2:]:
+            stage(unit)
 
     remote(total.at[pl.ds(0, 2)], back_near, ret_send.at[0], ret_recv.at[0], along(1)).wait()
     remote(total.at[pl.ds(2, 2)], back_far, ret_send.at[1], ret_recv.at[1], along(2)).wait()
@@ -432,7 +437,7 @@
     narrow = depth // 4
     wide = depth - narrow
     f32 = jnp.float32
-    units = CHUNKS + 4
+    units = CHUNKS + 5
     dma = pltpu.SemaphoreType.DMA
     xs = n_feat // 4
     far = (QUARTERS, CHUNKS, own // QUARTERS, rows)

time: 287 us -> 286 us (level)
  no operation moved by 1% of the time
where the time goes in v4:
time: 286 us
  Pallas kernels  284 us (99%)
    pallas_call x1, Pallas kernels, shards(): pl.pallas_call(kernel, out_shape=jax.ShapeDtypeStruct((STEPS, own, count)...  284 us

profile of v4, /device:TPU:1, one launch (start us, length us, event | category | flops | bytes accessed | tf_op | source)
XLA Modules:
  0.0 285.9 jit_solution(13787000499254179858)
XLA Ops:
  0.0 284.2 %shard_map.37 = f32[3,32,1024]{2,1,0:T(8,128)} custom-call(s32[3]{0:T(128)} %offsets.1, f32[1024,2048]{1,0:T(8,128)} %grads.1, f32[1,1024]{1,0:T(1,128)} %bitcast.1), custom_call_target="tpu_custom_call" | custom-call | tf_op jit(solution)/shard_map/pallas_call | solution.py:444
  284.2 1.8 copy.5
